TPU v7x, 512 devices: a whole 4x8x8 slice. The times are simulated.
512 devices in a mesh: utt: 8 (over x, core), tm: 64 (over y, z).
Axes of the slice: x: 4, y: 8, z: 8, core: 2. Of those that a mesh axis runs over, the one named last changes fastest.
Arguments:
- phone_ids: int32 [8, 4096], P('utt', 'tm'), may hold values from 0 to 255
- durations: int32 [8, 4096], P('utt'), may hold values from 1 to 16, 16384 in all within a row
- utt_lengths: int32 [8, 64], P('utt'), may hold values from 1 to 256, 4096 in all within a row
- utt_order: int32 [8, 64], P('utt'), may hold values from 0 to 63, each once within a row
- buckets: int32 [8, 64, 8], P('utt', 'tm'), may hold values from 0 to 7, each once within a row
- embed_table: bfloat16 [256, 384], replicated, may hold values from -6 to 6
- conv1_weight: bfloat16 [3456, 768], P(None, 'tm'), may hold values from -0.109375 to 0.109375
- conv2_weight: bfloat16 [384, 768], P(None, 'tm'), may hold values from -0.21875 to 0.21875
- norm_gain: float32 [384], replicated, may hold values from 0.1 to 1.9
- mel_weight: bfloat16 [384, 80], replicated, may hold values from -0.3125 to 0.3125
- pre_weight: bfloat16 [7, 80, 512], replicated, may hold values from -0.25 to 0.25
- up_weight: bfloat16 [512, 16, 256], P('tm'), may hold values from -0.1875 to 0.1875
Outputs:
- bucketed: bfloat16 [8, 64, 8, 256, 256], P('utt', 'tm')
All inputs are finite; a program needn't handle non-finite values.
Results may differ from a plain program's by a relative error of at most 0.0067.
Values may be sent and summed in bfloat16 or wider, within the bound.
A program may use at most 64 MiB of HBM per device.

v0:
```python
import jax
import jax.numpy as jnp
from jax import lax
from jax.sharding import PartitionSpec as P

F_DEV = 256
EPS = 1e-05


def padded(cells, sides, width):
    for axis, dim in sides:
        count = lax.axis_size(axis)
        ends = count - 1
        head = lax.slice_in_dim(cells, 0, width, axis=dim)
        tail = lax.slice_in_dim(cells, cells.shape[dim] - width, cells.shape[dim], axis=dim)
        cells = jnp.concatenate(
            [
                lax.ppermute(tail, axis, [(i, (i + 1) % count) for i in range(ends)]),
                cells,
                lax.ppermute(head, axis, [((i + 1) % count, i) for i in range(ends)]),
            ],
            axis=dim,
        )
    return cells


def utterance_of(indices, bounds):
    return jnp.sum((bounds[None, :] <= indices[:, None]).astype(jnp.int32), axis=1)


def frame_layout(lasting, lengths, ordering):
    phone_total = lasting.shape[0]
    utt_count = lengths.shape[0]
    phone_index = jnp.arange(phone_total, dtype=jnp.int32)
    bounds = jnp.cumsum(lengths)
    utt_first = bounds - lengths
    owners = utterance_of(phone_index, bounds)
    inclusive = jnp.cumsum(lasting)
    exclusive = inclusive - lasting
    first_frame = jnp.take(exclusive, utt_first)
    utt_frames = jnp.take(inclusive, bounds - 1) - first_frame
    slots = jnp.arange(utt_count, dtype=jnp.int32)
    places = jnp.sum(jnp.where(ordering[None, :] == slots[:, None], slots[None, :], 0), axis=1)
    offsets = jnp.sum(jnp.where(places[None, :] < places[:, None], utt_frames[None, :], 0), axis=1)
    starting = jnp.take(offsets, owners) + exclusive - jnp.take(first_frame, owners)
    return (starting, owners, bounds)


def masked_unfold(row_block, labels, offset, amount, width_taps, reach):
    center = labels[offset : offset + amount]
    columns = []
    for tap in range(width_taps):
        anchor = offset - reach + tap
        keep = (labels[anchor : anchor + amount] == center)[:, None]
        columns.append(
            jnp.where(keep, row_block[anchor : anchor + amount], jnp.zeros((), row_block.dtype))
        )
    return jnp.concatenate(columns, axis=1)


def shards(
    phone_ids,
    durations,
    utt_lengths,
    utt_order,
    buckets,
    embed_table,
    conv1_weight,
    conv2_weight,
    norm_gain,
    mel_weight,
    pre_weight,
    up_weight,
):
    phone_count = phone_ids.shape[1]
    device = lax.axis_index("tm")
    lasting = durations[0]
    starting, owners, bounds = frame_layout(lasting, utt_lengths[0], utt_order[0])
    ending = starting + lasting
    nearby = device * phone_count + jnp.arange(-4, phone_count + 4, dtype=jnp.int32)
    phone_labels = jnp.where(nearby < 0, -1, utterance_of(nearby, bounds))
    symbols = embed_table.shape[0]
    choose = (phone_ids[0][:, None] == jnp.arange(symbols, dtype=jnp.int32)[None, :]).astype(
        jnp.bfloat16
    )
    embedded = jnp.dot(choose, embed_table, preferred_element_type=jnp.float32).astype(jnp.bfloat16)
    widened = padded(embedded, (("tm", 0),), 4)
    unfolded = masked_unfold(widened, phone_labels, 4, phone_count, 9, 4)
    inward = lax.all_gather(conv1_weight, "tm", axis=1, tiled=True)
    outward = lax.all_gather(conv2_weight, "tm", axis=1, tiled=True)
    filters = jnp.maximum(
        jnp.dot(unfolded, inward, preferred_element_type=jnp.float32), 0.0
    ).astype(jnp.bfloat16)
    conv_out = lax.dot_general(
        filters, outward, (((1,), (1,)), ((), ())), preferred_element_type=jnp.float32
    )
    resid = embedded.astype(jnp.float32) + conv_out
    center = jnp.mean(resid, axis=1, keepdims=True)
    spread = jnp.mean((resid - center) ** 2, axis=1, keepdims=True)
    decoded = ((resid - center) * lax.rsqrt(spread + EPS) * norm_gain[None, :]).astype(jnp.bfloat16)
    span = F_DEV + 8
    frames = device * F_DEV - 4 + jnp.arange(span, dtype=jnp.int32)
    mel_width = mel_weight.shape[1]
    portion = lax.all_gather(decoded, "tm", axis=0, tiled=True)
    hit = (frames[:, None] >= starting[None, :]) & (frames[:, None] < ending[None, :])
    sums = jnp.dot(hit.astype(jnp.bfloat16), portion, preferred_element_type=jnp.float32)
    marks = jnp.sum(jnp.where(hit, owners[None, :] + 1, 0), axis=1)
    sums, marks = (sums, marks)
    mel_frames = jnp.dot(
        sums.astype(jnp.bfloat16), mel_weight, preferred_element_type=jnp.float32
    ).astype(jnp.bfloat16)
    frame_labels = marks - 1
    channels = pre_weight.shape[2]
    pre_flat = pre_weight.reshape(7 * mel_width, channels)
    columns = masked_unfold(mel_frames, frame_labels, 4, F_DEV, 7, 3)
    summed = jnp.dot(columns, pre_flat, preferred_element_type=jnp.float32)
    act_wide = padded(
        jnp.where(summed >= 0, summed, 0.1 * summed).astype(jnp.bfloat16), (("tm", 0),), 1
    )
    center_labels = frame_labels[4 : 4 + F_DEV]
    same_prev = (frame_labels[3 : 3 + F_DEV] == center_labels)[:, None]
    same_next = (frame_labels[5 : 5 + F_DEV] == center_labels)[:, None]
    act_mid = act_wide[1 : F_DEV + 1]
    act_prev = jnp.where(same_prev, act_wide[0:F_DEV], jnp.zeros((), jnp.bfloat16))
    act_next = jnp.where(same_next, act_wide[2 : F_DEV + 2], jnp.zeros((), jnp.bfloat16))
    out_width = up_weight.shape[2]
    groups = lax.axis_size("utt")
    placing = buckets[0, 0]
    selector = (placing[None, :] == jnp.arange(groups, dtype=jnp.int32)[:, None]).astype(
        jnp.bfloat16
    )
    portion = lax.all_gather(up_weight, "tm", axis=0, tiled=True)
    amount = portion.shape[0]
    weights = portion.reshape(amount, 16 * out_width)
    middle = jnp.dot(
        act_mid, weights[:, 4 * out_width : 12 * out_width], preferred_element_type=jnp.float32
    )
    before = jnp.dot(act_prev, weights[:, 12 * out_width :], preferred_element_type=jnp.float32)
    after = jnp.dot(act_next, weights[:, : 4 * out_width], preferred_element_type=jnp.float32)
    upsampled = middle + jnp.concatenate([before, after], axis=1)
    segments = upsampled.astype(jnp.bfloat16).reshape(groups, -1, out_width)
    outgoing = jnp.einsum(
        "bj,jsc->bsc", selector, segments, preferred_element_type=jnp.float32
    ).astype(jnp.bfloat16)
    arrived = lax.all_to_all(outgoing, "utt", split_axis=0, concat_axis=0, tiled=True)
    return arrived.reshape(1, 1, groups, -1, out_width)


def solution(mesh):
    placed = (
        P("utt", "tm"),
        P("utt", None),
        P("utt", None),
        P("utt", None),
        P("utt", "tm", None),
        P(),
        P(None, "tm"),
        P(None, "tm"),
        P(),
        P(),
        P(),
        P("tm", None, None),
    )
    return jax.shard_map(
        shards,
        mesh=mesh,
        in_specs=placed,
        out_specs=P("utt", "tm", None, None, None),
        check_vma=False,
    )
```

profile of v0, /device:TPU:1, one launch (start us, length us, event | category | flops | bytes accessed | tf_op | source)
XLA Modules:
  0.0 333.1 jit_solution(16332967862284316481)
XLA Ops:
  6.5 0.7 all-gather.10.cloned.1.call-update
  7.3 1.1 convolution_convert_fusion.1
  8.5 4.8 %collective-permute-start = (bf16[4,384]{1,0:T(4,128)(2,1)S(1)}, bf16[4,384]{1,0:T(4,128)(2,1)S(1)}, u32[]{:S(2)}, u32[]{:S(2)}) collective-permute-start(bf16[4,384]{1,0:T(4,128)(2,1)S(1)} %get-tuple-element.16), channel_id=1, source_target_pairs={{0,1},{1,2},{2,3},{3,4},{4,5},{5,6},{6,7},{7,8},{8,9},{9,10},{10,1... | collective-permute-start | bytes 9224 | tf_op jit(solution)/shard_map/ppermute | solution.py:18
  13.3 1.3 collective-permute-start.1
  14.6 0.7 copy.22
  15.3 0.1 reduce-window.21
  15.4 0.1 reduce
  15.6 0.1 convert_reduce_fusion.1
  15.7 0.1 slice_compare_fusion.6
  15.7 48.4 %all-gather.1 = bf16[64,12,384]{2,1,0:T(8,128)(2,1)S(1)} all-gather(bf16[1,12,384]{2,1,0:T(8,128)(2,1)} %bitcast.173), channel_id=1, replica_groups=mesh['utt'=8,'tm'=64] {'tm'}, dimensions={0}, use_global_device_ids=true | all-gather | bytes 599040 | tf_op jit(solution)/shard_map/all_gather | solution.py:90
  64.1 0.1 reshape.281
  64.3 0.1 fusion.43
  64.3 0.1 fusion.46
  64.4 0.1 fusion.40
  64.5 0.1 fusion.50
  64.6 0.1 fusion.34
  64.7 0.1 fusion.37
  64.8 0.1 fusion.31
  64.9 0.1 fusion.48
  65.0 44.1 %all-gather.10.cloned.1.call-done = bf16[64,12,3456]{2,1,0:T(8,128)(2,1)} async-done(((bf16[1,12,3456]{2,1,0:T(8,128)(2,1)}), bf16[64,12,3456]{2,1,0:T(8,128)(2,1)}) %all-gather.10.cloned.1.call-update) | async-done | bytes 5308432 | tf_op jit(solution)/shard_map/all_gather | solution.py:89
  109.1 9.2 %reshape.279 = bf16[768,3456]{1,0:T(8,128)(2,1)} reshape(bf16[64,12,3456]{2,1,0:T(8,128)(2,1)} %all-gather.10.cloned.1.call-done) | data formatting | bytes 10616832
  118.4 4.6 %fusion.79 = (f32[64]{0:T(128)S(1)}, f32[64,384]{1,0:T(8,128)S(1)}) fusion(bf16[768,384]{1,0:T(8,128)(2,1)S(1)} %reshape.281, bf16[64,3456]{1,0:T(8,128)(2,1)S(1)} %fusion.48, bf16[768,3456]{1,0:T(8,128)(2,1)} %reshape.279, bf16[64,384]{1,0:T(8,128)(2,1)S(1)} %convolution_convert_fusion.1), kind=kOutput, calls=%fused_computation.146 | convolution fusion | flops 377659328 | bytes 6488320 | tf_op jit(solution)/shard_map/dot_general | solution.py:94
  122.9 0.2 multiply_reduce_fusion
  123.1 0.7 multiply_convert_fusion
  123.9 0.7 all-gather.8.cloned.1.call-update
  124.6 0.3 reduce-window.19
  125.1 0.1 slice_reduce_fusion
  125.3 0.8 gather_fusion.1
  126.0 0.8 gather_fusion
  126.8 0.1 select_reduce_fusion.2
  127.0 0.2 select_reduce_fusion.1
  127.1 0.7 fusion.74
  127.8 0.7 fusion.78
  128.5 0.7 fusion.73
  129.2 0.7 fusion.72
  129.9 0.7 fusion.71
  130.6 0.7 fusion.76
  131.4 0.7 fusion.75
  132.1 0.7 fusion.77
  132.8 0.2 convert_reduce_fusion
  133.0 80.0 %fusion.67 = (s32[4096]{0:T(1024)S(1)}, s32[4096]{0:T(1024)S(1)}) fusion(s32[4096]{0:T(1024)S(1)} %bitcast.171, s32[]{:T(128)} %bitcast.135, s32[]{:T(128)} %bitcast.134, s32[]{:T(128)} %bitcast.133, s32[]{:T(128)} %bitcast.132, s32[]{:T(128)} %bitcast.131, s32[]{:T(128)} %bitcast.130, s32[]{:T(128)} %bitcast.129, s32[]{:T(128)} %bitcast.128, s32[]{:T(128)} %bitcast.127, ...), kind=kLoop, calls=%fused_computation.134 | loop fusion | flops 819200 | bytes 82432 | tf_op jit(solution)/shard_map/add | solution.py:79
  213.1 0.9 select_reduce_fusion
  214.1 3.4 %fusion.11 = bf16[264,80]{0,1:T(8,128)(2,1)S(1)} fusion(bf16[384,80]{0,1:T(8,128)(2,1)S(1)} %copy-done.5, bf16[4096,384]{1,0:T(8,128)(2,1)} %all-gather.6.cloned.1.call-done, s32[4096]{0:T(1024)S(1)} %get-tuple-element.6, s32[4096]{0:T(1024)S(1)} %get-tuple-element.8, s32[264]{0:T(512)S(1)} %iota_add_fusion), kind=kOutput, calls=%fused_computation.19 | convolution fusion | flops 850058880 | bytes 3283232 | tf_op jit(solution)/shard_map/dot_general | solution.py:109
  217.5 0.1 fusion.56
  217.6 0.1 fusion.55
  217.7 0.1 fusion.54
  217.8 0.1 slice_dynamic-update-slice_fusion
  217.9 0.1 fusion.53
  218.0 0.1 fusion.52
  218.0 0.1 fusion.51
  218.1 0.4 fusion.17
  218.6 1.3 collective-permute-start.2
  219.8 69.4 %all-gather.8.cloned.1.call-done = bf16[512,16,256]{2,1,0:T(8,128)(2,1)} async-done(((bf16[8,16,256]{2,1,0:T(8,128)(2,1)}), bf16[512,16,256]{2,1,0:T(8,128)(2,1)}) %all-gather.8.cloned.1.call-update) | async-done | bytes 4194320 | tf_op jit(solution)/shard_map/all_gather | solution.py:132
  289.2 4.4 %copy.25 = bf16[64,8,16,256]{3,1,2,0:T(8,128)(2,1)S(1)} copy(bf16[64,8,16,256]{3,2,1,0:T(8,128)(2,1)} %bitcast.164) | data formatting | bytes 8388608
  293.6 1.5 collective-permute-start.3
  295.1 0.5 fusion.14
  295.6 2.4 collective-permute-done.3
  298.0 0.5 fusion.12
  298.5 0.7 fusion.1
  299.2 0.5 reshape.114
  299.7 0.7 convolution_convert_fusion
  300.4 0.2 copy.24
  300.7 25.0 %all_to_all.5 = bf16[8,256,256]{2,1,0:T(8,128)(2,1)S(1)} all-to-all(bf16[8,256,256]{2,1,0:T(8,128)(2,1)S(1)} %copy.24), channel_id=1, replica_groups=mesh['utt'=8,'tm'=64] {'utt'}, dimensions={0} | all-to-all | bytes 2097152 | tf_op jit(solution)/shard_map/all_to_all | solution.py:145
  325.6 1.0 copy.43
  (39 shorter events, 0.5 us)
Async XLA Ops:
  6.5 211.6 %copy-start = (bf16[7,80,512]{2,1,0:T(8,128)(2,1)S(1)}, bf16[7,80,512]{2,1,0:T(8,128)(2,1)}, u32[]{:S(2)}) copy-start(bf16[7,80,512]{2,1,0:T(8,128)(2,1)} %param.26) | copy-start | bytes 1720324
  6.5 102.6 %all-gather.10.cloned.1.call-start = ((), (), s32[]{:S(2)}) async-start(), calls=%async_computation.3 | async-start | bytes 7188480 | tf_op jit(solution)/shard_map/all_gather | solution.py:89
  7.3 206.8 %all-gather.6.cloned.1.call-start = ((), (), s32[]{:S(2)}) async-start(), calls=%async_computation.1 | async-start | bytes 3194880 | tf_op jit(solution)/shard_map/all_gather | solution.py:104
  8.5 55.8 %collective-permute-start = (bf16[4,384]{1,0:T(4,128)(2,1)S(1)}, bf16[4,384]{1,0:T(4,128)(2,1)S(1)}, u32[]{:S(2)}, u32[]{:S(2)}) collective-permute-start(bf16[4,384]{1,0:T(4,128)(2,1)S(1)} %get-tuple-element.16), channel_id=1, source_target_pairs={{0,1},{1,2},{2,3},{3,4},{4,5},{5,6},{6,7},{7,8},{8,9},{9,10},{10,1... | collective-permute-start | bytes 9224 | tf_op jit(solution)/shard_map/ppermute | solution.py:18
  13.3 51.3 %collective-permute-start.1 = (bf16[4,384]{1,0:T(4,128)(2,1)S(1)}, bf16[4,384]{1,0:T(4,128)(2,1)S(1)}, u32[]{:S(2)}, u32[]{:S(2)}) collective-permute-start(bf16[4,384]{1,0:T(4,128)(2,1)S(1)} %get-tuple-element.15), channel_id=1, source_target_pairs={{1,0},{2,1},{3,2},{4,3},{5,4},{6,5},{7,6},{8,7},{9,8},{10,9},{11,1... | collective-permute-start | bytes 9224 | tf_op jit(solution)/shard_map/ppermute | solution.py:20
  118.3 4.8 %copy-start.2 = (f32[384]{0:T(512)S(1)}, f32[384]{0:T(512)}, u32[]{:S(2)}) copy-start(f32[384]{0:T(512)} %param.24) | copy-start | bytes 4612
  118.3 6.3 %copy-start.1 = (s32[1,4096]{1,0:T(1,128)S(1)}, s32[1,4096]{1,0:T(1,128)}, u32[]{:S(2)}) copy-start(s32[1,4096]{1,0:T(1,128)} %param.17) | copy-start | bytes 49156
  118.3 6.7 %copy-start.3 = (s32[1,64]{1,0:T(1,128)S(1)}, s32[1,64]{1,0:T(1,128)}, u32[]{:S(2)}) copy-start(s32[1,64]{1,0:T(1,128)} %param.18) | copy-start | bytes 772
  118.3 8.5 %copy-start.6 = (s32[1,64]{1,0:T(1,128)S(1)}, s32[1,64]{1,0:T(1,128)}, u32[]{:S(2)}) copy-start(s32[1,64]{1,0:T(1,128)} %param.19) | copy-start | bytes 772
  118.3 95.8 %copy-start.5 = (bf16[384,80]{0,1:T(8,128)(2,1)S(1)}, bf16[384,80]{0,1:T(8,128)(2,1)}, u32[]{:S(2)}) copy-start(bf16[384,80]{0,1:T(8,128)(2,1)} %param.25) | copy-start | bytes 184324
  123.9 165.4 %all-gather.8.cloned.1.call-start = ((), (), s32[]{:S(2)}) async-start(), calls=%async_computation.2 | async-start | bytes 4259840 | tf_op jit(solution)/shard_map/all_gather | solution.py:132
  218.6 76.6 %collective-permute-start.2 = (bf16[1,512]{1,0:T(2,128)(2,1)S(1)}, bf16[1,512]{1,0:T(2,128)(2,1)S(1)}, u32[]{:S(2)}, u32[]{:S(2)}) collective-permute-start(bf16[1,512]{1,0:T(2,128)(2,1)S(1)} %get-tuple-element.13), channel_id=1, source_target_pairs={{0,1},{1,2},{2,3},{3,4},{4,5},{5,6},{6,7},{7,8},{8,9},{9,10},{10,1... | collective-permute-start | bytes 3080 | tf_op jit(solution)/shard_map/ppermute | solution.py:18
  293.6 4.3 %collective-permute-start.3 = (bf16[1,512]{1,0:T(2,128)(2,1)S(1)}, bf16[1,512]{1,0:T(2,128)(2,1)S(1)}, u32[]{:S(2)}, u32[]{:S(2)}) collective-permute-start(bf16[1,512]{1,0:T(2,128)(2,1)S(1)} %get-tuple-element.14), channel_id=1, source_target_pairs={{1,0},{2,1},{3,2},{4,3},{5,4},{6,5},{7,6},{8,7},{9,8},{10,9},{11,1... | collective-permute-start | bytes 3080 | tf_op jit(solution)/shard_map/ppermute | solution.py:20
  298.5 1.3 copy-start.4
Sparse Core Ops, SparseCore 0:
  10.4 98.6 all-gather.9
  124.0 79.0 all-gather.5
  206.1 83.0 all-gather.7
where the time goes:
time: 335 us; the launch traced here: 333 us
  waiting for transfers between devices  117 us (35%)
  other arithmetic  84.5 us (25%)
  blocking collectives  73.4 us (22%)
  local copies, waits for them, and re-layouts  23.8 us (7%)
  between operations  13.5 us (4%)
  matrix products  11.9 us (4%)
  starting transfers between devices  8.95 us (3%)
    add x1, other arithmetic, shards(): ending = starting + lasting  80 us
    all_gather x1, waiting for transfers between devices, shards(): portion = lax.all_gather(up_weight, 'tm', axis=0, tiled=True)  69.4 us
    all_gather x1, blocking collectives, shards(): outward = lax.all_gather(conv2_weight, 'tm', axis=1, tiled=True)  48.4 us
    all_gather x1, waiting for transfers between devices, shards(): inward = lax.all_gather(conv1_weight, 'tm', axis=1, tiled=True)  44.1 us
    all_to_all x1, blocking collectives, shards(): lax.all_to_all(outgoing, 'utt', split_axis=0, concat_axis=0, tiled=True)  25 us
    unnamed x20, local copies, waits for them, and re-layouts  14.8 us
  transfers between devices with their start and end apart: 7, of which 3 were waited for; matrix products, arithmetic and copies ran while one was open for 31% of the time, Pallas kernels for 0%

commit v1 on v0

--- a/solution.py
+++ b/solution.py
@@ -5,6 +5,19 @@
 
 F_DEV = 256
 EPS = 1e-05
+
+
+def write_the_threads(u_in, row_axis, k_dim):
+    met_up = jnp.concatenate(
+        lax.all_to_all(
+            jnp.stack(lax.axis_size(row_axis) * [u_in], 0),
+            axis_name=row_axis,
+            split_axis=0,
+            concat_axis=0,
+        ),
+        k_dim,
+    )
+    return met_up
 
 
 def padded(cells, sides, width):
@@ -87,7 +100,7 @@
     widened = padded(embedded, (("tm", 0),), 4)
     unfolded = masked_unfold(widened, phone_labels, 4, phone_count, 9, 4)
     inward = lax.all_gather(conv1_weight, "tm", axis=1, tiled=True)
-    outward = lax.all_gather(conv2_weight, "tm", axis=1, tiled=True)
+    outward = write_the_threads(conv2_weight, "tm", 1)
     filters = jnp.maximum(
         jnp.dot(unfolded, inward, preferred_element_type=jnp.float32), 0.0
     ).astype(jnp.bfloat16)

time: 335 us -> 347 us (1.036)
  blocking collectives: 73.4 us -> 25 us
  waiting for transfers between devices: 117 us -> 159 us
  starting transfers between devices: 8.95 us -> 26.4 us
    all_gather x1 -> x0, blocking collectives: 48.4 us -> none  [shards(): outward = lax.all_gather(conv2_weight, 'tm', axis=1, tiled=True)]
    all_to_all x0 -> x1, waiting for transfers between devices: none -> 21 us  [write_the_threads(): lax.all_to_all(jnp.stack(lax.axis_size(row_axis) * [u_in], 0), axis_name=...]
    all_gather x1, waiting for transfers between devices: 44.1 us -> 64.5 us  [shards(): inward = lax.all_gather(conv1_weight, 'tm', axis=1, tiled=True)]
    all_to_all x0 -> x1, starting transfers between devices: none -> 17.5 us  [write_the_threads(): lax.all_to_all(jnp.stack(lax.axis_size(row_axis) * [u_in], 0), axis_name=...]
    unnamed x20 -> x19, local copies, waits for them, and re-layouts: 14.8 us -> 14.7 us
  transfers between devices with their start and end apart: 7 -> 8, of which waited for: 3 -> 4; matrix products, arithmetic and copies ran while one was open for 31% -> 30% of each run, Pallas kernels for 0% -> 0%
where the time goes in v1:
time: 347 us; the launch traced here: 345 us
  waiting for transfers between devices  159 us (46%)
  other arithmetic  84.5 us (24%)
  starting transfers between devices  26.4 us (8%)
  local copies, waits for them, and re-layouts  25.4 us (7%)
  blocking collectives  25 us (7%)
  between operations  13.5 us (4%)
  matrix products  11.9 us (3%)
    add x1, other arithmetic, shards(): ending = starting + lasting  80 us
    all_gather x1, waiting for transfers between devices, shards(): portion = lax.all_gather(up_weight, 'tm', axis=0, tiled=True)  69.4 us
    all_gather x1, waiting for transfers between devices, shards(): inward = lax.all_gather(conv1_weight, 'tm', axis=1, tiled=True)  64.5 us
    all_to_all x1, blocking collectives, shards(): lax.all_to_all(outgoing, 'utt', split_axis=0, concat_axis=0, tiled=True)  25 us
    all_to_all x1, waiting for transfers between devices, write_the_threads(): lax.all_to_all(jnp.stack(lax.axis_size(row_axis) * [u_in], 0), axis_name=...  21 us
    all_to_all x1, starting transfers between devices, write_the_threads(): lax.all_to_all(jnp.stack(lax.axis_size(row_axis) * [u_in], 0), axis_name=...  17.5 us
    unnamed x19, local copies, waits for them, and re-layouts  14.7 us
  transfers between devices with their start and end apart: 8, of which 4 were waited for; matrix products, arithmetic and copies ran while one was open for 30% of the time, Pallas kernels for 0%

profile of v1, /device:TPU:1, one launch (start us, length us, event | category | flops | bytes accessed | tf_op | source)
XLA Modules:
  0.0 345.4 jit_solution(12016876565271888409)
XLA Ops:
  6.5 0.7 all-gather.9.cloned.1.call-update
  7.3 1.1 convolution_convert_fusion.1
  8.4 4.8 %collective-permute-start = (bf16[4,384]{1,0:T(4,128)(2,1)S(1)}, bf16[4,384]{1,0:T(4,128)(2,1)S(1)}, u32[]{:S(2)}, u32[]{:S(2)}) collective-permute-start(bf16[4,384]{1,0:T(4,128)(2,1)S(1)} %get-tuple-element.16), channel_id=1, source_target_pairs={{0,1},{1,2},{2,3},{3,4},{4,5},{5,6},{6,7},{7,8},{8,9},{9,10},{10,1... | collective-permute-start | bytes 9224 | tf_op jit(solution)/shard_map/ppermute | solution.py:31
  13.2 1.3 collective-permute-start.1
  14.5 1.7 stack.2
  16.2 17.5 %all-to-all-start = ((bf16[64,384,12]{1,2,0:T(8,128)(2,1)}), bf16[64,384,12]{1,2,0:T(8,128)(2,1)S(1)}, u32[]{:S(2)}, u32[]{:S(2)}) async-start(bf16[64,384,12]{1,2,0:T(8,128)(2,1)} %stack.2), calls=%async_computation | async-start | bytes 1572864 | tf_op jit(solution)/shard_map/all_to_all | solution.py:12
  33.7 0.7 copy.23
  34.5 0.1 reduce-window.21
  34.6 0.1 reduce
  34.7 0.1 convert_reduce_fusion.1
  35.0 0.1 fusion.46
  35.1 0.1 fusion.40
  35.2 0.1 fusion.50
  35.3 0.1 fusion.34
  35.4 0.1 fusion.37
  35.5 0.1 fusion.31
  35.6 0.1 fusion.48
  35.7 21.0 %all-to-all-done = bf16[64,384,12]{1,2,0:T(8,128)(2,1)S(1)} async-done(((bf16[64,384,12]{1,2,0:T(8,128)(2,1)}), bf16[64,384,12]{1,2,0:T(8,128)(2,1)S(1)}, u32[]{:S(2)}, u32[]{:S(2)}) %all-to-all-start) | async-done | bytes 589856 | tf_op jit(solution)/shard_map/all_to_all | solution.py:12
  56.7 0.1 reshape.121
  56.8 64.5 %all-gather.9.cloned.1.call-done = bf16[64,12,3456]{2,1,0:T(8,128)(2,1)} async-done(((bf16[1,12,3456]{2,1,0:T(8,128)(2,1)}), bf16[64,12,3456]{2,1,0:T(8,128)(2,1)}) %all-gather.9.cloned.1.call-update) | async-done | bytes 5308432 | tf_op jit(solution)/shard_map/all_gather | solution.py:102
  121.3 9.2 %reshape.289 = bf16[768,3456]{1,0:T(8,128)(2,1)} reshape(bf16[64,12,3456]{2,1,0:T(8,128)(2,1)} %all-gather.9.cloned.1.call-done) | data formatting | bytes 10616832
  130.5 4.6 %fusion.79 = (f32[64]{0:T(128)S(1)}, f32[64,384]{1,0:T(8,128)S(1)}) fusion(bf16[384,768]{0,1:T(8,128)(2,1)S(1)} %reshape.121, bf16[64,3456]{1,0:T(8,128)(2,1)S(1)} %fusion.48, bf16[768,3456]{1,0:T(8,128)(2,1)} %reshape.289, bf16[64,384]{1,0:T(8,128)(2,1)S(1)} %convolution_convert_fusion.1), kind=kOutput, calls=%fused_computation.146 | convolution fusion | flops 377659328 | bytes 6488320 | tf_op jit(solution)/shard_map/dot_general | solution.py:107
  135.1 0.2 multiply_reduce_fusion
  135.3 0.7 multiply_convert_fusion
  136.1 0.7 all-gather.7.cloned.1.call-update
  136.8 0.3 reduce-window.19
  137.3 0.1 slice_reduce_fusion
  137.5 0.8 gather_fusion.1
  138.2 0.8 gather_fusion
  139.0 0.1 select_reduce_fusion.2
  139.1 0.2 select_reduce_fusion.1
  139.3 0.7 fusion.74
  140.0 0.7 fusion.78
  140.7 0.7 fusion.73
  141.4 0.7 fusion.72
  142.1 0.7 fusion.71
  142.8 0.7 fusion.76
  143.6 0.7 fusion.75
  144.3 0.7 fusion.77
  145.0 0.2 convert_reduce_fusion
  145.2 80.0 %fusion.67 = (s32[4096]{0:T(1024)S(1)}, s32[4096]{0:T(1024)S(1)}) fusion(s32[4096]{0:T(1024)S(1)} %bitcast.172, s32[]{:T(128)} %bitcast.135, s32[]{:T(128)} %bitcast.134, s32[]{:T(128)} %bitcast.133, s32[]{:T(128)} %bitcast.132, s32[]{:T(128)} %bitcast.131, s32[]{:T(128)} %bitcast.130, s32[]{:T(128)} %bitcast.129, s32[]{:T(128)} %bitcast.128, s32[]{:T(128)} %bitcast.127, ...), kind=kLoop, calls=%fused_computation.134 | loop fusion | flops 819200 | bytes 82432 | tf_op jit(solution)/shard_map/add | solution.py:92
  225.3 0.9 select_reduce_fusion
  226.3 3.4 fusion.11
  229.7 0.1 fusion.56
  229.8 0.1 fusion.55
  229.9 0.1 fusion.54
  230.0 0.1 slice_dynamic-update-slice_fusion
  230.0 0.1 fusion.53
  230.1 0.1 fusion.52
  230.2 0.1 fusion.51
  230.3 0.4 fusion.17
  230.7 1.3 collective-permute-start.2
  232.0 69.4 %all-gather.7.cloned.1.call-done = bf16[512,16,256]{2,1,0:T(8,128)(2,1)} async-done(((bf16[8,16,256]{2,1,0:T(8,128)(2,1)}), bf16[512,16,256]{2,1,0:T(8,128)(2,1)}) %all-gather.7.cloned.1.call-update) | async-done | bytes 4194320 | tf_op jit(solution)/shard_map/all_gather | solution.py:145
  301.4 4.4 %copy.26 = bf16[64,8,16,256]{3,1,2,0:T(8,128)(2,1)S(1)} copy(bf16[64,8,16,256]{3,2,1,0:T(8,128)(2,1)} %bitcast.164) | data formatting | bytes 8388608
  305.8 1.5 collective-permute-start.3
  307.3 0.5 fusion.14
  307.8 2.4 collective-permute-done.3
  310.2 0.5 fusion.12
  310.7 0.7 fusion.1
  311.4 0.5 reshape.124
  311.9 0.7 convolution_convert_fusion
  312.6 0.2 copy.25
  312.9 25.0 %all_to_all.10 = bf16[8,256,256]{2,1,0:T(8,128)(2,1)S(1)} all-to-all(bf16[8,256,256]{2,1,0:T(8,128)(2,1)S(1)} %copy.25), channel_id=1, replica_groups=mesh['utt'=8,'tm'=64] {'utt'}, dimensions={0} | all-to-all | bytes 2097152 | tf_op jit(solution)/shard_map/all_to_all | solution.py:158
  337.9 1.0 copy.44
  (41 shorter events, 0.7 us)
Async XLA Ops:
  6.5 223.8 %copy-start = (bf16[7,80,512]{2,1,0:T(8,128)(2,1)S(1)}, bf16[7,80,512]{2,1,0:T(8,128)(2,1)}, u32[]{:S(2)}) copy-start(bf16[7,80,512]{2,1,0:T(8,128)(2,1)} %param.26) | copy-start | bytes 1720324
  6.5 114.7 %all-gather.9.cloned.1.call-start = ((), (), s32[]{:S(2)}) async-start(), calls=%async_computation.4 | async-start | bytes 7188480 | tf_op jit(solution)/shard_map/all_gather | solution.py:102
  8.4 26.5 %collective-permute-start = (bf16[4,384]{1,0:T(4,128)(2,1)S(1)}, bf16[4,384]{1,0:T(4,128)(2,1)S(1)}, u32[]{:S(2)}, u32[]{:S(2)}) collective-permute-start(bf16[4,384]{1,0:T(4,128)(2,1)S(1)} %get-tuple-element.16), channel_id=1, source_target_pairs={{0,1},{1,2},{2,3},{3,4},{4,5},{5,6},{6,7},{7,8},{8,9},{9,10},{10,1... | collective-permute-start | bytes 9224 | tf_op jit(solution)/shard_map/ppermute | solution.py:31
  13.2 22.0 %collective-permute-start.1 = (bf16[4,384]{1,0:T(4,128)(2,1)S(1)}, bf16[4,384]{1,0:T(4,128)(2,1)S(1)}, u32[]{:S(2)}, u32[]{:S(2)}) collective-permute-start(bf16[4,384]{1,0:T(4,128)(2,1)S(1)} %get-tuple-element.15), channel_id=1, source_target_pairs={{1,0},{2,1},{3,2},{4,3},{5,4},{6,5},{7,6},{8,7},{9,8},{10,9},{11,1... | collective-permute-start | bytes 9224 | tf_op jit(solution)/shard_map/ppermute | solution.py:33
  16.2 40.5 %all-to-all-start = ((bf16[64,384,12]{1,2,0:T(8,128)(2,1)}), bf16[64,384,12]{1,2,0:T(8,128)(2,1)S(1)}, u32[]{:S(2)}, u32[]{:S(2)}) async-start(bf16[64,384,12]{1,2,0:T(8,128)(2,1)} %stack.2), calls=%async_computation | async-start | bytes 1572864 | tf_op jit(solution)/shard_map/all_to_all | solution.py:12
  33.7 192.6 %all-gather.5.cloned.1.call-start = ((), (), s32[]{:S(2)}) async-start(), calls=%async_computation.2 | async-start | bytes 3194880 | tf_op jit(solution)/shard_map/all_gather | solution.py:117
  130.5 4.8 %copy-start.2 = (f32[384]{0:T(512)S(1)}, f32[384]{0:T(512)}, u32[]{:S(2)}) copy-start(f32[384]{0:T(512)} %param.24) | copy-start | bytes 4612
  130.5 6.3 %copy-start.1 = (s32[1,4096]{1,0:T(1,128)S(1)}, s32[1,4096]{1,0:T(1,128)}, u32[]{:S(2)}) copy-start(s32[1,4096]{1,0:T(1,128)} %param.17) | copy-start | bytes 49156
  130.5 6.7 %copy-start.3 = (s32[1,64]{1,0:T(1,128)S(1)}, s32[1,64]{1,0:T(1,128)}, u32[]{:S(2)}) copy-start(s32[1,64]{1,0:T(1,128)} %param.18) | copy-start | bytes 772
  130.5 8.5 %copy-start.6 = (s32[1,64]{1,0:T(1,128)S(1)}, s32[1,64]{1,0:T(1,128)}, u32[]{:S(2)}) copy-start(s32[1,64]{1,0:T(1,128)} %param.19) | copy-start | bytes 772
  130.5 95.8 %copy-start.5 = (bf16[384,80]{0,1:T(8,128)(2,1)S(1)}, bf16[384,80]{0,1:T(8,128)(2,1)}, u32[]{:S(2)}) copy-start(bf16[384,80]{0,1:T(8,128)(2,1)} %param.25) | copy-start | bytes 184324
  136.1 165.4 %all-gather.7.cloned.1.call-start = ((), (), s32[]{:S(2)}) async-start(), calls=%async_computation.3 | async-start | bytes 4259840 | tf_op jit(solution)/shard_map/all_gather | solution.py:145
  230.7 76.6 %collective-permute-start.2 = (bf16[1,512]{1,0:T(2,128)(2,1)S(1)}, bf16[1,512]{1,0:T(2,128)(2,1)S(1)}, u32[]{:S(2)}, u32[]{:S(2)}) collective-permute-start(bf16[1,512]{1,0:T(2,128)(2,1)S(1)} %get-tuple-element.13), channel_id=1, source_target_pairs={{0,1},{1,2},{2,3},{3,4},{4,5},{5,6},{6,7},{7,8},{8,9},{9,10},{10,1... | collective-permute-start | bytes 3080 | tf_op jit(solution)/shard_map/ppermute | solution.py:31
  305.8 4.3 %collective-permute-start.3 = (bf16[1,512]{1,0:T(2,128)(2,1)S(1)}, bf16[1,512]{1,0:T(2,128)(2,1)S(1)}, u32[]{:S(2)}, u32[]{:S(2)}) collective-permute-start(bf16[1,512]{1,0:T(2,128)(2,1)S(1)} %get-tuple-element.14), channel_id=1, source_target_pairs={{1,0},{2,1},{3,2},{4,3},{5,4},{6,5},{7,6},{8,7},{9,8},{10,9},{11,1... | collective-permute-start | bytes 3080 | tf_op jit(solution)/shard_map/ppermute | solution.py:33
  310.7 1.3 copy-start.4
Sparse Core Ops, SparseCore 0:
  10.4 110.8 all-gather.8
  136.2 79.0 all-gather.4
  218.3 83.0 all-gather.6
